TPU v7x, 512 devices: a whole 4x4x16 slice. The times are simulated.
512 devices in a mesh: section: 8 (over x_lo, y), seq: 64 (over x_hi, z, core).
Axes of the slice: x: 4 (x_hi: 2, x_lo: 2; x = x_hi * 2 + x_lo), y: 4, z: 16, core: 2. Of those that a mesh axis runs over, the one named last changes fastest.
Arguments:
- resident_microbatches: bfloat16 [8, 8192, 1024], P('section', 'seq'), may hold values from -64 to 64
- arriving_microbatch: bfloat16 [8192, 1024], P('seq'), may hold values from -64 to 64
- prenormal_scaling: float32 [8, 1024], P('section'), may hold values from 0.1 to 1.9
- attention_triple_matrix: bfloat16 [8, 1024, 3072], P('section', 'seq'), may hold values from -0.1875 to 0.1875
- exit_projection_matrix: bfloat16 [8, 1024, 1024], P('section'), may hold values from -0.1875 to 0.1875
- mirrored_lookup_tile: int32 [64, 4], replicated, may hold values from 0 to 1
Outputs:
- tick_out: bfloat16 [2, 8, 8192, 1024], P(None, 'section', 'seq')
All inputs are finite; a program needn't handle non-finite values.
Results may differ from a plain program's by a relative error of at most 0.004.
Values may be sent and summed in bfloat16 or wider, within the bound.
A program may use at most 64 MiB of HBM per device.

v0:
```python
import jax
import jax.numpy as jnp
from jax import lax
from jax.sharding import PartitionSpec as P

HEADS = 8
HEAD = 128
BLOCK = 64
LEVELS = 4
epsilon = 1e-06


def swapped(x, axis, stride):
    return lax.ppermute(x, axis, [(i, i ^ 1 << stride) for i in range(lax.axis_size(axis))])


def from_behind(block, axis, distance):
    devices = range(lax.axis_size(axis))
    route = [(i - distance, i) for i in devices if i - distance in devices]
    return lax.ppermute(block, axis, route)


def head_norm(projected, row_count):
    shaped = projected.reshape(row_count, HEADS, HEAD)
    mean_square = jnp.mean(shaped * shaped, axis=-1, keepdims=True)
    return (shaped * lax.rsqrt(mean_square + epsilon)).astype(jnp.bfloat16)


def transform_through_tier(
    hidden_in, gain_row, weights, out_weights, mirrored_lookup_tile, compute_unit
):
    row_count = hidden_in.shape[0]
    blocks = row_count // BLOCK
    inner_width = HEADS * HEAD
    widened = hidden_in.astype(jnp.float32)
    mean_square = jnp.mean(widened * widened, axis=-1, keepdims=True)
    normed = (widened * lax.rsqrt(mean_square + epsilon) * gain_row).astype(jnp.bfloat16)
    projected = jnp.dot(normed, weights, preferred_element_type=jnp.float32)
    queries = head_norm(projected[:, :inner_width], row_count)
    key_rows = head_norm(projected[:, inner_width : 2 * inner_width], row_count).reshape(
        row_count, inner_width
    )
    values = projected[:, 2 * inner_width :].astype(jnp.bfloat16)
    key_value = jnp.stack([key_rows, values])
    remote = []
    for bit_level in range(LEVELS):
        arrived = swapped(key_value, "seq", bit_level)
        wanted = mirrored_lookup_tile[compute_unit, bit_level]
        remote.append(lax.dynamic_slice_in_dim(arrived, wanted * BLOCK, BLOCK, 1))
    remote = jnp.concatenate(remote, axis=1)
    far_keys = jnp.broadcast_to(
        remote[0].reshape(1, LEVELS * BLOCK, HEADS, HEAD), (blocks, LEVELS * BLOCK, HEADS, HEAD)
    )
    far_values = jnp.broadcast_to(
        remote[1].reshape(1, LEVELS * BLOCK, HEADS, HEAD), (blocks, LEVELS * BLOCK, HEADS, HEAD)
    )
    query_blocks = queries.reshape(blocks, BLOCK, HEADS, HEAD)
    all_keys = jnp.concatenate([key_rows.reshape(blocks, BLOCK, HEADS, HEAD), far_keys], axis=1)
    all_values = jnp.concatenate([values.reshape(blocks, BLOCK, HEADS, HEAD), far_values], axis=1)
    score_scale = HEAD ** (-0.5)
    scores = (
        jnp.einsum("cqhd,ckhd->chqk", query_blocks, all_keys, preferred_element_type=jnp.float32)
        * score_scale
    )
    exps = jnp.exp(scores)
    weights_soft = (exps / jnp.sum(exps, axis=-1, keepdims=True)).astype(jnp.bfloat16)
    mixed_heads = jnp.einsum(
        "chqk,ckhd->cqhd", weights_soft, all_values, preferred_element_type=jnp.float32
    )
    attended = mixed_heads.astype(jnp.bfloat16).reshape(row_count, inner_width)
    return (widened + jnp.dot(attended, out_weights, preferred_element_type=jnp.float32)).astype(
        jnp.bfloat16
    )


def per_device(
    resident_microbatches,
    arriving_microbatch,
    prenormal_scaling,
    attention_triple_matrix,
    exit_projection_matrix,
    mirrored_lookup_tile,
):
    layer_parameters = lax.all_gather(attention_triple_matrix[0], "seq", axis=0, tiled=True)
    compute_unit = lax.axis_index("seq")
    section_index = lax.axis_index("section")
    starting_result = transform_through_tier(
        resident_microbatches[0],
        prenormal_scaling[0],
        layer_parameters,
        exit_projection_matrix[0],
        mirrored_lookup_tile,
        compute_unit,
    )
    moved = from_behind(starting_result, "section", 1)
    second_in = jnp.where(section_index == 0, arriving_microbatch, moved)
    second_out = transform_through_tier(
        second_in,
        prenormal_scaling[0],
        layer_parameters,
        exit_projection_matrix[0],
        mirrored_lookup_tile,
        compute_unit,
    )
    return jnp.stack([starting_result, second_out])[:, None]


def solution(mesh):
    placed = (
        P("section", "seq", None),
        P("seq", None),
        P("section", None),
        P("section", "seq", None),
        P("section", None, None),
        P(),
    )
    return jax.shard_map(
        per_device,
        mesh=mesh,
        in_specs=placed,
        out_specs=P(None, "section", "seq", None),
        check_vma=False,
    )
```

profile of v0, /device:TPU:34, one launch (start us, length us, event | category | flops | bytes accessed | tf_op | source)
XLA Modules:
  0.0 360.5 jit_solution(13483647688169495418)
XLA Ops:
  6.5 0.7 all-gather.3.cloned.1.call-update
  7.3 1.1 fusion.54
  8.4 163.1 %all-gather.3.cloned.1.call-done = bf16[1,1024,3072]{2,1,0:T(8,128)(2,1)} async-done(((bf16[1,16,3072]{2,1,0:T(8,128)(2,1)}), bf16[1,1024,3072]{2,1,0:T(8,128)(2,1)}) %all-gather.3.cloned.1.call-update) | async-done | bytes 6291472 | tf_op jit(solution)/shard_map/all_gather | solution.py:84
  171.4 3.9 %fusion.2 = f32[128,3072]{1,0:T(8,128)S(1)} fusion(bf16[1,1024,3072]{2,1,0:T(8,128)(2,1)} %all-gather.3.cloned.1.call-done, bf16[1,128,1024]{2,1,0:T(8,128)(2,1)} %param.6, f32[1024]{0:T(1024)} %bitcast.157, f32[128]{0:T(128)S(1)} %add_rsqrt_fusion.5), kind=kOutput, calls=%fused_computation.2 | convolution fusion | flops 805830656 | bytes 8131072 | tf_op jit(solution)/shard_map/dot_general | solution.py:38
  175.4 1.1 copy-done.2
  176.7 0.2 reduce_sum.73
  177.1 0.2 mul.156
  177.3 2.4 multiply_bitcast_fusion.2
  179.7 0.9 pad_maximum_fusion.2
  180.6 3.5 collective-permute-start.2
  184.1 0.7 constant_dynamic-slice_fusion.8
  187.3 2.3 collective-permute-start.1
  189.6 1.9 collective-permute-start
  191.5 5.1 %collective-permute-start.3 = (bf16[2,128,1024]{2,1,0:T(8,128)(2,1)}, bf16[2,128,1024]{2,1,0:T(8,128)(2,1)}, u32[]{:S(2)}, u32[]{:S(2)}) collective-permute-start(bf16[2,128,1024]{2,1,0:T(8,128)(2,1)} %pad_maximum_fusion.2), channel_id=1, source_target_pairs={{0,8},{1,9},{2,10},{3,11},{4,12},{5,13},{6,14},{7,15},{8,0},{9,1},... | collective-permute-start | bytes 1572872 | tf_op jit(solution)/shard_map/ppermute | solution.py:14
  196.6 1.1 copy.82
  197.7 0.2 reduce_sum.74
  198.1 1.2 copy.83
  199.5 0.8 copy.61
  200.2 0.2 fusion.61
  200.5 7.2 %collective-permute-done.2 = bf16[2,128,1024]{2,1,0:T(8,128)(2,1)} collective-permute-done((bf16[2,128,1024]{2,1,0:T(8,128)(2,1)}, bf16[2,128,1024]{2,1,0:T(8,128)(2,1)}, u32[]{:S(2)}, u32[]{:S(2)}) %collective-permute-start.2) | collective-permute-done | bytes 524320 | tf_op jit(solution)/shard_map/ppermute | solution.py:14
  207.7 1.0 constant_dynamic-slice_fusion.5
  208.6 12.4 %collective-permute-done.1 = bf16[2,128,1024]{2,1,0:T(8,128)(2,1)} collective-permute-done((bf16[2,128,1024]{2,1,0:T(8,128)(2,1)}, bf16[2,128,1024]{2,1,0:T(8,128)(2,1)}, u32[]{:S(2)}, u32[]{:S(2)}) %collective-permute-start.1) | collective-permute-done | bytes 524320 | tf_op jit(solution)/shard_map/ppermute | solution.py:14
  221.0 1.0 constant_dynamic-slice_fusion.6
  222.0 1.0 constant_dynamic-slice_fusion.7
  223.0 25.9 %collective-permute-done.3 = bf16[2,128,1024]{2,1,0:T(8,128)(2,1)} collective-permute-done((bf16[2,128,1024]{2,1,0:T(8,128)(2,1)}, bf16[2,128,1024]{2,1,0:T(8,128)(2,1)}, u32[]{:S(2)}, u32[]{:S(2)}) %collective-permute-start.3) | collective-permute-done | bytes 524320 | tf_op jit(solution)/shard_map/ppermute | solution.py:14
  248.9 1.0 constant_dynamic-slice_fusion.4
  250.4 0.2 broadcast_in_dim.42
  250.6 1.8 multiply_exponential_fusion.1
  252.4 0.2 broadcast_in_dim.19
  252.6 3.2 fusion.43
  255.8 1.1 copy.68
  256.9 0.4 fusion.37
  257.4 3.5 collective-permute-start.4
  260.9 7.8 %collective-permute-done.4 = bf16[128,1024]{1,0:T(8,128)(2,1)S(1)} collective-permute-done((bf16[128,1024]{1,0:T(8,128)(2,1)S(1)}, bf16[128,1024]{1,0:T(8,128)(2,1)S(1)}, u32[]{:S(2)}, u32[]{:S(2)}) %collective-permute-start.4) | collective-permute-done | bytes 262176 | tf_op jit(solution)/shard_map/ppermute | solution.py:20
  268.9 3.8 %fusion = f32[128,3072]{1,0:T(8,128)S(1)} fusion(bf16[1,1024,3072]{2,1,0:T(8,128)(2,1)} %all-gather.3.cloned.1.call-done, bf16[128,1024]{1,0:T(8,128)(2,1)S(1)} %get-tuple-element.6, f32[128]{0:T(128)S(1)} %add_rsqrt_fusion.4, f32[1024]{0:T(1024)S(1)} %bitcast.158), kind=kOutput, calls=%fused_computation | convolution fusion | flops 805830656 | bytes 8131072 | tf_op jit(solution)/shard_map/dot_general | solution.py:38
  272.8 1.1 copy-done.1
  273.9 0.9 fusion.82
  274.9 0.2 reduce_sum.77
  275.3 0.2 mul.180
  275.5 2.2 multiply_bitcast_fusion
  277.8 0.8 pad_maximum_fusion.3
  278.6 1.9 collective-permute-start.7
  280.5 2.0 collective-permute-start.6
  282.5 1.9 collective-permute-start.5
  284.6 0.2 reduce_sum.78
  284.9 8.3 %collective-permute-start.8 = (bf16[2,128,1024]{2,1,0:T(8,128)(2,1)}, bf16[2,128,1024]{2,1,0:T(8,128)(2,1)}, u32[]{:S(2)}, u32[]{:S(2)}) collective-permute-start(bf16[2,128,1024]{2,1,0:T(8,128)(2,1)} %pad_maximum_fusion.3), channel_id=1, source_target_pairs={{0,8},{1,9},{2,10},{3,11},{4,12},{5,13},{6,14},{7,15},{8,0},{9,1},... | collective-permute-start | bytes 1572872 | tf_op jit(solution)/shard_map/ppermute | solution.py:14
  293.2 1.1 copy.92
  294.6 1.0 copy.96
  295.6 0.8 copy.72
  296.3 0.2 fusion.59
  296.5 8.6 %collective-permute-done.7 = bf16[2,128,1024]{2,1,0:T(8,128)(2,1)} collective-permute-done((bf16[2,128,1024]{2,1,0:T(8,128)(2,1)}, bf16[2,128,1024]{2,1,0:T(8,128)(2,1)}, u32[]{:S(2)}, u32[]{:S(2)}) %collective-permute-start.7) | collective-permute-done | bytes 524320 | tf_op jit(solution)/shard_map/ppermute | solution.py:14
  305.1 1.0 constant_dynamic-slice_fusion.1
  306.1 1.0 constant_dynamic-slice_fusion.2
  307.1 1.0 constant_dynamic-slice_fusion.3
  308.0 35.8 %collective-permute-done.8 = bf16[2,128,1024]{2,1,0:T(8,128)(2,1)} collective-permute-done((bf16[2,128,1024]{2,1,0:T(8,128)(2,1)}, bf16[2,128,1024]{2,1,0:T(8,128)(2,1)}, u32[]{:S(2)}, u32[]{:S(2)}) %collective-permute-start.8) | collective-permute-done | bytes 524320 | tf_op jit(solution)/shard_map/ppermute | solution.py:14
  343.9 1.0 constant_dynamic-slice_fusion
  345.4 0.2 broadcast_in_dim.46
  345.6 1.8 multiply_exponential_fusion
  347.4 0.2 broadcast_in_dim.44
  347.6 3.2 fusion.46
  350.7 1.1 copy.79
  351.9 0.4 fusion.40
  352.3 0.5 copy-done.6
  352.8 0.8 maximum_bitcast_fusion
  (63 shorter events, 2.7 us)
Async XLA Ops:
  6.5 250.4 %copy-start = (bf16[1,1024,1024]{2,1,0:T(8,128)(2,1)S(1)}, bf16[1,1024,1024]{2,1,0:T(8,128)(2,1)}, u32[]{:S(2)}) copy-start(bf16[1,1024,1024]{2,1,0:T(8,128)(2,1)} %param.10) | copy-start | bytes 6291460
  6.5 164.9 %all-gather.3.cloned.1.call-start = ((), (), s32[]{:S(2)}) async-start(), calls=%async_computation | async-start | bytes 6389760 | tf_op jit(solution)/shard_map/all_gather | solution.py:84
  175.4 1.1 copy-start.2
  177.3 6.8 %copy-start.9 = (s32[64,4]{0,1:T(4,128)S(1)}, s32[64,4]{0,1:T(4,128)}, u32[]{:S(2)}) copy-start(s32[64,4]{0,1:T(4,128)} %param.11) | copy-start | bytes 3076
  180.6 27.1 %collective-permute-start.2 = (bf16[2,128,1024]{2,1,0:T(8,128)(2,1)}, bf16[2,128,1024]{2,1,0:T(8,128)(2,1)}, u32[]{:S(2)}, u32[]{:S(2)}) collective-permute-start(bf16[2,128,1024]{2,1,0:T(8,128)(2,1)} %pad_maximum_fusion.2), channel_id=1, source_target_pairs={{0,4},{1,5},{2,6},{3,7},{4,0},{5,1},{6,2},{7,3},{8,12},{9,13},{10,... | collective-permute-start | bytes 1572872 | tf_op jit(solution)/shard_map/ppermute | solution.py:14
  187.3 33.8 %collective-permute-start.1 = (bf16[2,128,1024]{2,1,0:T(8,128)(2,1)}, bf16[2,128,1024]{2,1,0:T(8,128)(2,1)}, u32[]{:S(2)}, u32[]{:S(2)}) collective-permute-start(bf16[2,128,1024]{2,1,0:T(8,128)(2,1)} %pad_maximum_fusion.2), channel_id=1, source_target_pairs={{0,2},{1,3},{2,0},{3,1},{4,6},{5,7},{6,4},{7,5},{8,10},{9,11},{10,... | collective-permute-start | bytes 1572872 | tf_op jit(solution)/shard_map/ppermute | solution.py:14
  189.6 32.4 %collective-permute-start = (bf16[2,128,1024]{2,1,0:T(8,128)(2,1)}, bf16[2,128,1024]{2,1,0:T(8,128)(2,1)}, u32[]{:S(2)}, u32[]{:S(2)}) collective-permute-start(bf16[2,128,1024]{2,1,0:T(8,128)(2,1)} %pad_maximum_fusion.2), channel_id=1, source_target_pairs={{0,1},{1,0},{2,3},{3,2},{4,5},{5,4},{6,7},{7,6},{8,9},{9,8},{10,11... | collective-permute-start | bytes 1572872 | tf_op jit(solution)/shard_map/ppermute | solution.py:14
  191.5 57.4 %collective-permute-start.3 = (bf16[2,128,1024]{2,1,0:T(8,128)(2,1)}, bf16[2,128,1024]{2,1,0:T(8,128)(2,1)}, u32[]{:S(2)}, u32[]{:S(2)}) collective-permute-start(bf16[2,128,1024]{2,1,0:T(8,128)(2,1)} %pad_maximum_fusion.2), channel_id=1, source_target_pairs={{0,8},{1,9},{2,10},{3,11},{4,12},{5,13},{6,14},{7,15},{8,0},{9,1},... | collective-permute-start | bytes 1572872 | tf_op jit(solution)/shard_map/ppermute | solution.py:14
  252.6 4.4 %copy-start.3 = (bf16[1,128,1024]{2,1,0:T(8,128)(2,1)S(1)}, bf16[1,128,1024]{2,1,0:T(8,128)(2,1)}, u32[]{:S(2)}) copy-start(bf16[1,128,1024]{2,1,0:T(8,128)(2,1)} %param.6) | copy-start | bytes 786436
  256.9 11.8 %copy-start.7 = (bf16[128,1024]{1,0:T(8,128)(2,1)S(1)}, bf16[128,1024]{1,0:T(8,128)(2,1)}, u32[]{:S(2)}) copy-start(bf16[128,1024]{1,0:T(8,128)(2,1)} %param.7) | copy-start | bytes 786436
  256.9 12.0 %copy-start.8 = (f32[1,1024]{1,0:T(1,128)S(1)}, f32[1,1024]{1,0:T(1,128)}, u32[]{:S(2)}) copy-start(f32[1,1024]{1,0:T(1,128)} %param.8) | copy-start | bytes 12292
  257.4 15.4 %copy-start.5 = (bf16[128,1024]{1,0:T(8,128)(2,1)}, bf16[128,1024]{1,0:T(8,128)(2,1)S(1)}, u32[]{:S(2)}) copy-start(bf16[128,1024]{1,0:T(8,128)(2,1)S(1)} %fusion.37) | copy-start | bytes 786436
  257.4 11.3 %collective-permute-start.4 = (bf16[128,1024]{1,0:T(8,128)(2,1)S(1)}, bf16[128,1024]{1,0:T(8,128)(2,1)S(1)}, u32[]{:S(2)}, u32[]{:S(2)}) collective-permute-start(bf16[128,1024]{1,0:T(8,128)(2,1)S(1)} %fusion.37), channel_id=1, source_target_pairs={{0,64},{64,128},{128,192},{192,256},{256,320},{320,384},{384,448},... | collective-permute-start | bytes 786440 | tf_op jit(solution)/shard_map/ppermute | solution.py:20
  272.8 1.2 copy-start.1
  275.5 2.3 copy-start.4
  278.6 26.5 %collective-permute-start.7 = (bf16[2,128,1024]{2,1,0:T(8,128)(2,1)}, bf16[2,128,1024]{2,1,0:T(8,128)(2,1)}, u32[]{:S(2)}, u32[]{:S(2)}) collective-permute-start(bf16[2,128,1024]{2,1,0:T(8,128)(2,1)} %pad_maximum_fusion.3), channel_id=1, source_target_pairs={{0,4},{1,5},{2,6},{3,7},{4,0},{5,1},{6,2},{7,3},{8,12},{9,13},{10,... | collective-permute-start | bytes 1572872 | tf_op jit(solution)/shard_map/ppermute | solution.py:14
  280.5 25.5 %collective-permute-start.6 = (bf16[2,128,1024]{2,1,0:T(8,128)(2,1)}, bf16[2,128,1024]{2,1,0:T(8,128)(2,1)}, u32[]{:S(2)}, u32[]{:S(2)}) collective-permute-start(bf16[2,128,1024]{2,1,0:T(8,128)(2,1)} %pad_maximum_fusion.3), channel_id=1, source_target_pairs={{0,2},{1,3},{2,0},{3,1},{4,6},{5,7},{6,4},{7,5},{8,10},{9,11},{10,... | collective-permute-start | bytes 1572872 | tf_op jit(solution)/shard_map/ppermute | solution.py:14
  282.5 24.5 %collective-permute-start.5 = (bf16[2,128,1024]{2,1,0:T(8,128)(2,1)}, bf16[2,128,1024]{2,1,0:T(8,128)(2,1)}, u32[]{:S(2)}, u32[]{:S(2)}) collective-permute-start(bf16[2,128,1024]{2,1,0:T(8,128)(2,1)} %pad_maximum_fusion.3), channel_id=1, source_target_pairs={{0,1},{1,0},{2,3},{3,2},{4,5},{5,4},{6,7},{7,6},{8,9},{9,8},{10,11... | collective-permute-start | bytes 1572872 | tf_op jit(solution)/shard_map/ppermute | solution.py:14
  284.9 59.0 %collective-permute-start.8 = (bf16[2,128,1024]{2,1,0:T(8,128)(2,1)}, bf16[2,128,1024]{2,1,0:T(8,128)(2,1)}, u32[]{:S(2)}, u32[]{:S(2)}) collective-permute-start(bf16[2,128,1024]{2,1,0:T(8,128)(2,1)} %pad_maximum_fusion.3), channel_id=1, source_target_pairs={{0,8},{1,9},{2,10},{3,11},{4,12},{5,13},{6,14},{7,15},{8,0},{9,1},... | collective-permute-start | bytes 1572872 | tf_op jit(solution)/shard_map/ppermute | solution.py:14
  351.9 1.0 copy-start.6
Sparse Core Ops, SparseCore 0:
  10.6 160.7 all-gather.2
where the time goes:
time: 362 us; the launch traced here: 360 us
  waiting for transfers between devices  261 us (72%)
  starting transfers between devices  30.4 us (8%)
  local copies, waits for them, and re-layouts  23.6 us (7%)
  matrix products  18.6 us (5%)
  between operations  16.4 us (5%)
  other arithmetic  9.93 us (3%)
    all_gather x1, waiting for transfers between devices, per_device(): lax.all_gather(attention_triple_matrix[0], 'seq', axis=0, tiled=True)  163 us
    ppermute x8, waiting for transfers between devices, swapped(): lax.ppermute(x, axis, [(i, i ^ 1 << stride) for i in range(lax.axis_size(...  89.9 us
    ppermute x8, starting transfers between devices, swapped(): lax.ppermute(x, axis, [(i, i ^ 1 << stride) for i in range(lax.axis_size(...  27 us
    unnamed x38, local copies, waits for them, and re-layouts  9.15 us
    ppermute x1, waiting for transfers between devices, from_behind(): return lax.ppermute(block, axis, route)  7.83 us
    dynamic_slice x8, local copies, waits for them, and re-layouts, transform_through_tier(): remote.append(lax.dynamic_slice_in_dim(arrived, wanted * BLOCK, BLOCK, 1))  7.78 us
    dot_general x2, matrix products, transform_through_tier(): projected = jnp.dot(normed, weights, preferred_element_type=jnp.float32)  7.77 us
  transfers between devices with their start and end apart: 10, of which 7 were waited for; matrix products, arithmetic and copies ran while one was open for 4% of the time, Pallas kernels for 0%

commit v1 on v0

--- a/solution.py
+++ b/solution.py
@@ -81,7 +81,10 @@
     exit_projection_matrix,
     mirrored_lookup_tile,
 ):
-    layer_parameters = lax.all_gather(attention_triple_matrix[0], "seq", axis=0, tiled=True)
+    layer_parameters = jnp.concatenate(
+        lax.all_to_all(jnp.stack([attention_triple_matrix[0]] * lax.axis_size("seq")), "seq", 0, 0),
+        axis=0,
+    )
     compute_unit = lax.axis_index("seq")
     section_index = lax.axis_index("section")
     starting_result = transform_through_tier(

time: 362 us -> 482 us (1.33)
  the two profiles are of different devices: /device:TPU:34 before, /device:TPU:167 now
where the time goes in v1:
time: 482 us; the launch traced here: 481 us
  waiting for transfers between devices  363 us (75%)
  starting transfers between devices  57.6 us (12%)
  local copies, waits for them, and re-layouts  30 us (6%)
  matrix products  18.6 us (4%)
  other arithmetic  8.98 us (2%)
    all_to_all x1, waiting for transfers between devices, per_device(): lax.all_to_all(jnp.stack([attention_triple_matrix[0]] * lax.axis_size('se...  274 us
    ppermute x8, waiting for transfers between devices, swapped(): lax.ppermute(x, axis, [(i, i ^ 1 << stride) for i in range(lax.axis_size(...  82.8 us
    ppermute x8, starting transfers between devices, swapped(): lax.ppermute(x, axis, [(i, i ^ 1 << stride) for i in range(lax.axis_size(...  37.3 us
    all_to_all x1, starting transfers between devices, per_device(): lax.all_to_all(jnp.stack([attention_triple_matrix[0]] * lax.axis_size('se...  17.1 us
    unnamed x40, local copies, waits for them, and re-layouts  11.1 us
  transfers between devices with their start and end apart: 10, of which 6 were waited for; matrix products, arithmetic and copies ran while one was open for 3% of the time, Pallas kernels for 0%

profile of v1, /device:TPU:167, one launch (start us, length us, event | category | flops | bytes accessed | tf_op | source)
XLA Modules:
  0.0 481.3 jit_solution(403139046214456172)
XLA Ops:
  0.0 4.5 stack.24
  4.5 17.1 %all-to-all-start = ((bf16[64,16,3072]{2,1,0:T(8,128)(2,1)}), bf16[64,16,3072]{2,1,0:T(8,128)(2,1)}, u32[]{:S(2)}, u32[]{:S(2)}) async-start(bf16[64,16,3072]{2,1,0:T(8,128)(2,1)} %stack.24), calls=%async_computation | async-start | bytes 12582912 | tf_op jit(solution)/shard_map/all_to_all | solution.py:85
  21.7 274.3 %all-to-all-done = bf16[64,16,3072]{2,1,0:T(8,128)(2,1)} async-done(((bf16[64,16,3072]{2,1,0:T(8,128)(2,1)}), bf16[64,16,3072]{2,1,0:T(8,128)(2,1)}, u32[]{:S(2)}, u32[]{:S(2)}) %all-to-all-start) | async-done | bytes 6291488 | tf_op jit(solution)/shard_map/all_to_all | solution.py:85
  296.1 3.8 fusion.67
  299.9 0.9 fusion.79
  300.8 0.3 copy-done.2
  301.3 0.2 reduce_sum.73
  301.7 0.2 mul.160
  301.9 2.4 multiply_bitcast_fusion.2
  304.3 0.9 pad_maximum_fusion.2
  305.2 2.5 collective-permute-start.3
  307.7 0.7 constant_dynamic-slice_fusion.8
  310.9 1.9 collective-permute-start.2
  312.8 3.1 collective-permute-start.1
  315.9 5.4 %collective-permute-start = (bf16[2,128,1024]{2,1,0:T(8,128)(2,1)}, bf16[2,128,1024]{2,1,0:T(8,128)(2,1)}, u32[]{:S(2)}, u32[]{:S(2)}) collective-permute-start(bf16[2,128,1024]{2,1,0:T(8,128)(2,1)} %pad_maximum_fusion.2), channel_id=1, source_target_pairs={{0,1},{1,0},{2,3},{3,2},{4,5},{5,4},{6,7},{7,6},{8,9},{9,8},{10,11... | collective-permute-start | bytes 1572872 | tf_op jit(solution)/shard_map/ppermute | solution.py:14
  321.3 1.1 copy.82
  322.4 0.2 reduce_sum.74
  322.8 1.0 copy.87
  323.8 0.7 copy.61
  324.6 1.1 copy.83
  325.7 0.9 copy.81
  326.7 0.2 fusion.58
  326.9 20.2 %collective-permute-done.3 = bf16[2,128,1024]{2,1,0:T(8,128)(2,1)} collective-permute-done((bf16[2,128,1024]{2,1,0:T(8,128)(2,1)}, bf16[2,128,1024]{2,1,0:T(8,128)(2,1)}, u32[]{:S(2)}, u32[]{:S(2)}) %collective-permute-start.3) | collective-permute-done | bytes 524320 | tf_op jit(solution)/shard_map/ppermute | solution.py:14
  347.1 1.0 constant_dynamic-slice_fusion.4
  348.1 1.0 constant_dynamic-slice_fusion.5
  349.1 17.5 %collective-permute-done.1 = bf16[2,128,1024]{2,1,0:T(8,128)(2,1)} collective-permute-done((bf16[2,128,1024]{2,1,0:T(8,128)(2,1)}, bf16[2,128,1024]{2,1,0:T(8,128)(2,1)}, u32[]{:S(2)}, u32[]{:S(2)}) %collective-permute-start.1) | collective-permute-done | bytes 524320 | tf_op jit(solution)/shard_map/ppermute | solution.py:14
  366.6 1.0 constant_dynamic-slice_fusion.6
  367.6 1.0 constant_dynamic-slice_fusion.7
  369.1 0.2 broadcast_in_dim.42
  369.3 0.8 copy-done.4
  370.0 1.8 multiply_exponential_fusion.1
  372.0 3.2 fusion.39
  375.2 1.1 copy.68
  376.4 0.4 fusion.33
  376.8 3.2 collective-permute-start.4
  380.0 6.0 %collective-permute-done.4 = bf16[128,1024]{1,0:T(8,128)(2,1)S(1)} collective-permute-done((bf16[128,1024]{1,0:T(8,128)(2,1)S(1)}, bf16[128,1024]{1,0:T(8,128)(2,1)S(1)}, u32[]{:S(2)}, u32[]{:S(2)}) %collective-permute-start.4) | collective-permute-done | bytes 262176 | tf_op jit(solution)/shard_map/ppermute | solution.py:20
  386.3 3.8 fusion.64
  390.1 1.0 fusion.81
  391.1 0.4 copy-done.1
  391.6 0.2 reduce_sum.77
  392.0 0.2 mul.185
  392.2 2.2 multiply_bitcast_fusion
  394.5 0.8 pad_maximum_fusion.3
  395.3 4.5 collective-permute-start.8
  399.8 11.5 %collective-permute-start.7 = (bf16[2,128,1024]{2,1,0:T(8,128)(2,1)}, bf16[2,128,1024]{2,1,0:T(8,128)(2,1)}, u32[]{:S(2)}, u32[]{:S(2)}) collective-permute-start(bf16[2,128,1024]{2,1,0:T(8,128)(2,1)} %pad_maximum_fusion.3), channel_id=1, source_target_pairs={{0,4},{1,5},{2,6},{3,7},{4,0},{5,1},{6,2},{7,3},{8,12},{9,13},{10,... | collective-permute-start | bytes 1572872 | tf_op jit(solution)/shard_map/ppermute | solution.py:14
  411.3 4.1 collective-permute-start.6
  415.4 4.2 collective-permute-start.5
  419.8 0.2 reduce_sum.78
  420.1 1.0 copy.96
  421.2 0.8 copy.72
  422.0 1.1 copy.90
  423.3 0.2 fusion.56
  423.5 13.4 %collective-permute-done.8 = bf16[2,128,1024]{2,1,0:T(8,128)(2,1)} collective-permute-done((bf16[2,128,1024]{2,1,0:T(8,128)(2,1)}, bf16[2,128,1024]{2,1,0:T(8,128)(2,1)}, u32[]{:S(2)}, u32[]{:S(2)}) %collective-permute-start.8) | collective-permute-done | bytes 524320 | tf_op jit(solution)/shard_map/ppermute | solution.py:14
  436.8 1.0 constant_dynamic-slice_fusion
  437.8 1.0 constant_dynamic-slice_fusion.1
  438.8 31.7 %collective-permute-done.6 = bf16[2,128,1024]{2,1,0:T(8,128)(2,1)} collective-permute-done((bf16[2,128,1024]{2,1,0:T(8,128)(2,1)}, bf16[2,128,1024]{2,1,0:T(8,128)(2,1)}, u32[]{:S(2)}, u32[]{:S(2)}) %collective-permute-start.6) | collective-permute-done | bytes 524320 | tf_op jit(solution)/shard_map/ppermute | solution.py:14
  470.5 1.0 constant_dynamic-slice_fusion.2
  471.5 1.0 constant_dynamic-slice_fusion.3
  473.2 1.8 multiply_exponential_fusion
  475.1 3.2 fusion.42
  478.4 1.1 copy.79
  479.5 0.4 fusion.36
  480.0 0.5 copy-done.7
  480.5 0.8 maximum_bitcast_fusion
  (65 shorter events, 3.1 us)
Async XLA Ops:
  0.0 376.4 %copy-start = (bf16[1,1024,1024]{2,1,0:T(8,128)(2,1)S(1)}, bf16[1,1024,1024]{2,1,0:T(8,128)(2,1)}, u32[]{:S(2)}) copy-start(bf16[1,1024,1024]{2,1,0:T(8,128)(2,1)} %param.10) | copy-start | bytes 6291460
  4.5 17.1 %copy-start.3 = (bf16[1,128,1024]{2,1,0:T(8,128)(2,1)S(1)}, bf16[1,128,1024]{2,1,0:T(8,128)(2,1)}, u32[]{:S(2)}) copy-start(bf16[1,128,1024]{2,1,0:T(8,128)(2,1)} %param.6) | copy-start | bytes 786436
  4.5 291.6 %copy-start.9 = (f32[1,1024]{1,0:T(1,128)S(1)}, f32[1,1024]{1,0:T(1,128)}, u32[]{:S(2)}) copy-start(f32[1,1024]{1,0:T(1,128)} %param.8) | copy-start | bytes 12292
  4.5 291.6 %all-to-all-start = ((bf16[64,16,3072]{2,1,0:T(8,128)(2,1)}), bf16[64,16,3072]{2,1,0:T(8,128)(2,1)}, u32[]{:S(2)}, u32[]{:S(2)}) async-start(bf16[64,16,3072]{2,1,0:T(8,128)(2,1)} %stack.24), calls=%async_computation | async-start | bytes 12582912 | tf_op jit(solution)/shard_map/all_to_all | solution.py:85
  299.9 1.2 copy-start.2
  301.9 5.8 %copy-start.10 = (s32[64,4]{0,1:T(4,128)S(1)}, s32[64,4]{0,1:T(4,128)}, u32[]{:S(2)}) copy-start(s32[64,4]{0,1:T(4,128)} %param.11) | copy-start | bytes 3076
  305.2 41.9 %collective-permute-start.3 = (bf16[2,128,1024]{2,1,0:T(8,128)(2,1)}, bf16[2,128,1024]{2,1,0:T(8,128)(2,1)}, u32[]{:S(2)}, u32[]{:S(2)}) collective-permute-start(bf16[2,128,1024]{2,1,0:T(8,128)(2,1)} %pad_maximum_fusion.2), channel_id=1, source_target_pairs={{0,8},{1,9},{2,10},{3,11},{4,12},{5,13},{6,14},{7,15},{8,0},{9,1},... | collective-permute-start | bytes 1572872 | tf_op jit(solution)/shard_map/ppermute | solution.py:14
  310.9 37.2 %collective-permute-start.2 = (bf16[2,128,1024]{2,1,0:T(8,128)(2,1)}, bf16[2,128,1024]{2,1,0:T(8,128)(2,1)}, u32[]{:S(2)}, u32[]{:S(2)}) collective-permute-start(bf16[2,128,1024]{2,1,0:T(8,128)(2,1)} %pad_maximum_fusion.2), channel_id=1, source_target_pairs={{0,4},{1,5},{2,6},{3,7},{4,0},{5,1},{6,2},{7,3},{8,12},{9,13},{10,... | collective-permute-start | bytes 1572872 | tf_op jit(solution)/shard_map/ppermute | solution.py:14
  312.8 53.8 %collective-permute-start.1 = (bf16[2,128,1024]{2,1,0:T(8,128)(2,1)}, bf16[2,128,1024]{2,1,0:T(8,128)(2,1)}, u32[]{:S(2)}, u32[]{:S(2)}) collective-permute-start(bf16[2,128,1024]{2,1,0:T(8,128)(2,1)} %pad_maximum_fusion.2), channel_id=1, source_target_pairs={{0,2},{1,3},{2,0},{3,1},{4,6},{5,7},{6,4},{7,5},{8,10},{9,11},{10,... | collective-permute-start | bytes 1572872 | tf_op jit(solution)/shard_map/ppermute | solution.py:14
  315.9 51.7 %collective-permute-start = (bf16[2,128,1024]{2,1,0:T(8,128)(2,1)}, bf16[2,128,1024]{2,1,0:T(8,128)(2,1)}, u32[]{:S(2)}, u32[]{:S(2)}) collective-permute-start(bf16[2,128,1024]{2,1,0:T(8,128)(2,1)} %pad_maximum_fusion.2), channel_id=1, source_target_pairs={{0,1},{1,0},{2,3},{3,2},{4,5},{5,4},{6,7},{7,6},{8,9},{9,8},{10,11... | collective-permute-start | bytes 1572872 | tf_op jit(solution)/shard_map/ppermute | solution.py:14
  369.0 1.0 copy-start.4
  376.4 9.7 %copy-start.8 = (bf16[128,1024]{1,0:T(8,128)(2,1)S(1)}, bf16[128,1024]{1,0:T(8,128)(2,1)}, u32[]{:S(2)}) copy-start(bf16[128,1024]{1,0:T(8,128)(2,1)} %param.7) | copy-start | bytes 786436
  376.8 13.3 %copy-start.6 = (bf16[128,1024]{1,0:T(8,128)(2,1)}, bf16[128,1024]{1,0:T(8,128)(2,1)S(1)}, u32[]{:S(2)}) copy-start(bf16[128,1024]{1,0:T(8,128)(2,1)S(1)} %fusion.33) | copy-start | bytes 786436
  376.8 9.2 %collective-permute-start.4 = (bf16[128,1024]{1,0:T(8,128)(2,1)S(1)}, bf16[128,1024]{1,0:T(8,128)(2,1)S(1)}, u32[]{:S(2)}, u32[]{:S(2)}) collective-permute-start(bf16[128,1024]{1,0:T(8,128)(2,1)S(1)} %fusion.33), channel_id=1, source_target_pairs={{0,64},{64,128},{128,192},{192,256},{256,320},{320,384},{384,448},... | collective-permute-start | bytes 786440 | tf_op jit(solution)/shard_map/ppermute | solution.py:20
  390.1 1.4 copy-start.1
  392.2 2.3 copy-start.5
  395.3 41.5 %collective-permute-start.8 = (bf16[2,128,1024]{2,1,0:T(8,128)(2,1)}, bf16[2,128,1024]{2,1,0:T(8,128)(2,1)}, u32[]{:S(2)}, u32[]{:S(2)}) collective-permute-start(bf16[2,128,1024]{2,1,0:T(8,128)(2,1)} %pad_maximum_fusion.3), channel_id=1, source_target_pairs={{0,8},{1,9},{2,10},{3,11},{4,12},{5,13},{6,14},{7,15},{8,0},{9,1},... | collective-permute-start | bytes 1572872 | tf_op jit(solution)/shard_map/ppermute | solution.py:14
  399.8 38.0 %collective-permute-start.7 = (bf16[2,128,1024]{2,1,0:T(8,128)(2,1)}, bf16[2,128,1024]{2,1,0:T(8,128)(2,1)}, u32[]{:S(2)}, u32[]{:S(2)}) collective-permute-start(bf16[2,128,1024]{2,1,0:T(8,128)(2,1)} %pad_maximum_fusion.3), channel_id=1, source_target_pairs={{0,4},{1,5},{2,6},{3,7},{4,0},{5,1},{6,2},{7,3},{8,12},{9,13},{10,... | collective-permute-start | bytes 1572872 | tf_op jit(solution)/shard_map/ppermute | solution.py:14
  411.3 59.2 %collective-permute-start.6 = (bf16[2,128,1024]{2,1,0:T(8,128)(2,1)}, bf16[2,128,1024]{2,1,0:T(8,128)(2,1)}, u32[]{:S(2)}, u32[]{:S(2)}) collective-permute-start(bf16[2,128,1024]{2,1,0:T(8,128)(2,1)} %pad_maximum_fusion.3), channel_id=1, source_target_pairs={{0,2},{1,3},{2,0},{3,1},{4,6},{5,7},{6,4},{7,5},{8,10},{9,11},{10,... | collective-permute-start | bytes 1572872 | tf_op jit(solution)/shard_map/ppermute | solution.py:14
  415.4 56.0 %collective-permute-start.5 = (bf16[2,128,1024]{2,1,0:T(8,128)(2,1)}, bf16[2,128,1024]{2,1,0:T(8,128)(2,1)}, u32[]{:S(2)}, u32[]{:S(2)}) collective-permute-start(bf16[2,128,1024]{2,1,0:T(8,128)(2,1)} %pad_maximum_fusion.3), channel_id=1, source_target_pairs={{0,1},{1,0},{2,3},{3,2},{4,5},{5,4},{6,7},{7,6},{8,9},{9,8},{10,11... | collective-permute-start | bytes 1572872 | tf_op jit(solution)/shard_map/ppermute | solution.py:14
  479.5 1.0 copy-start.7
